TPU v7x, 256 devices: a whole 4x4x8 slice. The times are simulated.
256 devices in a mesh: expert: 16 (over y, x), tensor: 16 (over z, core).
Axes of the slice: x: 4, y: 4, z: 8, core: 2. Of those that a mesh axis runs over, the one named last changes fastest.
Arguments:
- queries: bfloat16 [4096, 8192], P('expert', 'tensor'), may hold values from -8 to 8
- keys_values: bfloat16 [16, 4, 1280, 256], P('expert'), may hold values from -6 to 6
- prefix_len: int32 [16], P('expert'), may hold values from 128 to 1024, as said below
- out_proj: bfloat16 [8192, 4096], P('tensor', 'expert'), may hold values from -0.0625 to 0.0625
- residual: bfloat16 [4096, 4096], P(('expert', 'tensor')), may hold values from -1.796875 to 1.796875
- norm_gain: float32 [4096], replicated, may hold values from 0.1 to 1.9
- expert_ids: int32 [4096, 8], P('expert'), may hold values from 0 to 63, all different within a row; in each aligned block of 16 rows (0 to 15, 16 to 31, ...) at most 3 rows name the same one
- route_weights: bfloat16 [4096, 8], P('expert'), may hold values from 0.19921875 to 1
- w_gate: bfloat16 [256, 4096, 384], P(('expert', 'tensor')), may hold values from -0.09375 to 0.09375
- w_up: bfloat16 [256, 4096, 384], P(('expert', 'tensor')), may hold values from -0.09375 to 0.09375
- w_down: bfloat16 [256, 384, 4096], P(('expert', 'tensor')), may hold values from -0.15625 to 0.15625
Outputs:
- layer_out: bfloat16 [4096, 4096], P(('expert', 'tensor'))
Inputs may be any that keep to these rules, and one draw needn't show every extreme that they name: `expert_ids`: in the rows of one device (aligned blocks of 16 rows) no expert is named by more than 3 rows, a bound that some block reaches; a row names 8 different experts. `prefix_len`: some sequence has all 1024 slots live.
All inputs are finite; a program needn't handle non-finite values.
Results may differ from a plain program's by a relative error of at most 0.035.
Values may be sent and summed in bfloat16 or wider, within the bound.
No kernel may reach another device: no remote copies, remote signals or barrier semaphores. Data moves between devices by JAX's collectives and lax.ppermute only.
A program may use at most 128 MiB of HBM per device.

v0:
```python
import math
import jax
import jax.numpy as jnp
from jax import lax
from jax.sharding import PartitionSpec as P

HEADS = 64
KVH = 4
HD = 128
TOPK = 8
HSPLIT = 4
TOK_DEV = 16
PREFIX = 1024


def norm_rows(hidden_state, norm_gain):
    values = hidden_state.astype(jnp.float32)
    factor = lax.rsqrt(jnp.mean(values * values, axis=-1, keepdims=True) + 1e-06)
    return (values * factor * norm_gain[None, :]).astype(jnp.bfloat16)


def route_tables(expert_ids, route_weights, experts, most_rows):
    total_rows = expert_ids.shape[0]
    named_mask = expert_ids[:, :, None] == jnp.arange(experts, dtype=jnp.int32)[None, None, :]
    hit_table = jnp.sum(named_mask.astype(jnp.int32), axis=1)
    weight_table = jnp.sum(
        jnp.where(named_mask, route_weights[:, :, None].astype(jnp.float32), 0.0), axis=1
    )
    grouped = hit_table.reshape(total_rows // TOK_DEV, TOK_DEV, experts)
    rank_table = (jnp.cumsum(grouped, axis=1) - grouped).reshape(total_rows, experts)
    share_index = (jnp.arange(total_rows, dtype=jnp.int32) // TOK_DEV)[:, None]
    position_table = share_index * most_rows + rank_table
    return (hit_table, weight_table, rank_table, position_table)


def pick_slot(table, expert_count, slot_count, slot_index):
    shaped = table.reshape(table.shape[0], expert_count, slot_count)
    return lax.dynamic_index_in_dim(shaped, slot_index, 2, keepdims=False)


def shards(
    queries,
    keys_values,
    prefix_len,
    out_proj,
    residual,
    norm_gain,
    expert_ids,
    route_weights,
    w_gate,
    w_up,
    w_down,
):
    tensor_count = lax.axis_size("tensor")
    expert_count = lax.axis_size("expert")
    tensor_index = lax.axis_index("tensor")
    step_rows = queries.shape[0]
    per_device = queries.shape[1] // HD
    group_size = HEADS // KVH
    kv_index = tensor_index * per_device // group_size
    cached = lax.dynamic_index_in_dim(keys_values[0], kv_index, 0, keepdims=False)
    key_rows = cached[:, :HD]
    value_rows = cached[:, HD:]
    context = cached.shape[0]
    query_rows = queries.reshape(step_rows, per_device, HD)
    scores = jnp.einsum(
        "nhd,cd->hnc", query_rows, key_rows, preferred_element_type=jnp.float32
    ) / math.sqrt(HD)
    columns = jnp.arange(context, dtype=jnp.int32)[None, :]
    positions = jnp.arange(step_rows, dtype=jnp.int32)[:, None]
    visible = ((columns < prefix_len[0]) | (columns >= PREFIX) & (columns - PREFIX <= positions))[
        None
    ]
    highest = jnp.max(jnp.where(visible, scores, -1e30), axis=-1, keepdims=True)
    weights = jnp.exp(jnp.where(visible, scores - highest, -1e30))
    summed = jnp.sum(weights, axis=-1)
    blended = jnp.einsum(
        "hnc,cd->nhd", weights.astype(jnp.bfloat16), value_rows, preferred_element_type=jnp.float32
    )
    attended = (
        (blended / jnp.transpose(summed)[:, :, None])
        .astype(jnp.bfloat16)
        .reshape(step_rows, per_device * HD)
    )
    head_part = jnp.dot(
        attended,
        lax.all_gather(out_proj, "expert", axis=1, tiled=True),
        preferred_element_type=jnp.float32,
    )
    slot_count = tensor_count // HSPLIT
    experts = expert_count * slot_count
    most_rows = min(TOK_DEV, max(2, TOK_DEV * TOPK // experts + 1))
    capacity = tensor_count * most_rows
    slot_index = tensor_index // HSPLIT
    start_row = tensor_index * TOK_DEV
    hit_table, weight_table, rank_table, position_table = route_tables(
        expert_ids, route_weights, experts, most_rows
    )
    hit_slot = pick_slot(hit_table, expert_count, slot_count, slot_index)
    weight_slot = pick_slot(weight_table, expert_count, slot_count, slot_index)
    position_slot = pick_slot(position_table, expert_count, slot_count, slot_index)
    slot_match = (hit_slot[:, :, None] == 1) & (
        position_slot[:, :, None] == jnp.arange(capacity, dtype=jnp.int32)[None, None, :]
    )
    head_sum = lax.psum(head_part.astype(jnp.bfloat16), "tensor").astype(jnp.float32)
    residual_full = lax.all_gather(residual, "tensor", axis=0, tiled=True)
    state_full = (residual_full.astype(jnp.float32) + head_sum).astype(jnp.bfloat16)
    hidden_state = lax.dynamic_slice_in_dim(state_full, start_row, TOK_DEV, 0)
    normed_full = norm_rows(state_full, norm_gain)
    source_rows = jnp.sum(
        jnp.where(slot_match, jnp.arange(step_rows, dtype=jnp.int32)[:, None, None], 0), axis=0
    )
    filled = jnp.any(slot_match, axis=0)
    outgoing = jnp.where(
        filled[:, :, None], jnp.take(normed_full, source_rows, axis=0), jnp.zeros((), jnp.bfloat16)
    )
    arrived_rows = lax.all_to_all(outgoing, "expert", split_axis=0, concat_axis=0, tiled=True)
    flat_rows = arrived_rows.reshape(-1, arrived_rows.shape[-1])
    gate_val = jnp.dot(flat_rows, w_gate[0], preferred_element_type=jnp.float32)
    up_val = jnp.dot(flat_rows, w_up[0], preferred_element_type=jnp.float32)
    inner = (jax.nn.silu(gate_val) * up_val).astype(jnp.bfloat16)
    result = jnp.dot(inner, w_down[0], preferred_element_type=jnp.float32).astype(jnp.bfloat16)
    computed = result.reshape(arrived_rows.shape)
    returned = lax.all_to_all(computed, "expert", split_axis=0, concat_axis=0, tiled=True)
    combine_weights = jnp.where(slot_match, weight_slot[:, :, None], 0.0).astype(jnp.bfloat16)
    expert_part = jnp.einsum(
        "njc,jcd->nd", combine_weights, returned, preferred_element_type=jnp.float32
    )
    expert_share = lax.psum_scatter(
        expert_part.astype(jnp.bfloat16), "tensor", scatter_dimension=0, tiled=True
    ).astype(jnp.float32)
    return (hidden_state.astype(jnp.float32) + expert_share).astype(jnp.bfloat16)


def solution(mesh):
    return jax.shard_map(
        shards,
        mesh=mesh,
        in_specs=(
            P("expert", "tensor"),
            P("expert", None, None, None),
            P("expert"),
            P("tensor", "expert"),
            P(("expert", "tensor"), None),
            P(),
            P("expert", None),
            P("expert", None),
            P(("expert", "tensor"), None, None),
            P(("expert", "tensor"), None, None),
            P(("expert", "tensor"), None, None),
        ),
        out_specs=P(("expert", "tensor"), None),
        check_vma=False,
    )
```

profile of v0, /device:TPU:2, one launch (start us, length us, event | category | flops | bytes accessed | tf_op | source)
XLA Modules:
  0.0 520.2 jit_solution(15658658182001831944)
XLA Ops:
  6.5 0.0 copy-start
  6.5 0.0 all-gather.5.cloned.1.call-start
  6.5 0.7 all-gather.5.cloned.1.call-update
  7.3 0.0 all-gather.3.cloned.1.call-start
  7.3 0.7 all-gather.3.cloned.1.call-update
  8.0 0.0 all-reduce.2.cloned.1.call-start
  8.1 0.8 convert_reduce_fusion
  8.9 0.1 copy.36
  9.7 1.1 copy.38
  10.7 1.9 reduce_window_sum.14
  12.7 2.0 dynamic-slice_bitcast_fusion
  14.7 1.0 fusion.26
  15.7 5.1 fusion.62
  20.8 2.4 fusion.33
  23.2 51.8 %all-gather.5.cloned.1.call-done = bf16[512,4096]{1,0:T(8,128)(2,1)} async-done(((bf16[512,256]{1,0:T(8,128)(2,1)}), bf16[512,4096]{1,0:T(8,128)(2,1)}) %all-gather.5.cloned.1.call-update) | async-done | bytes 4194320 | tf_op jit(solution)/shard_map/all_gather | solution.py:87
  75.0 4.8 convolution_convert_fusion.1
  79.8 0.0 all-reduce.2.cloned.1.call-update
  79.8 0.9 fusion.57
  80.8 0.4 select_reduce_fusion
  81.2 0.1 reshape.155
  81.2 0.4 fusion.37
  81.6 34.7 %all-gather.3.cloned.1.call-done = bf16[256,4096]{1,0:T(8,128)(2,1)} async-done(((bf16[16,4096]{1,0:T(8,128)(2,1)}), bf16[256,4096]{1,0:T(8,128)(2,1)}) %all-gather.3.cloned.1.call-update) | async-done | bytes 2097168 | tf_op jit(solution)/shard_map/all_gather | solution.py:106
  116.4 115.7 %all-reduce.2.cloned.1.call-done = bf16[256,4096]{1,0:T(8,128)(2,1)} async-done(((bf16[256,4096]{1,0:T(8,128)(2,1)}), bf16[256,4096]{1,0:T(8,128)(2,1)}) %all-reduce.2.cloned.1.call-update) | async-done | bytes 2097168 | tf_op jit(solution)/shard_map/psum | solution.py:105
  232.1 3.2 fusion.6
  235.2 0.0 copy-start.1
  235.3 1.3 copy-done.1
  236.6 0.0 copy-done.3
  236.6 2.0 fusion.8
  238.6 13.8 %gather_fusion = bf16[768,4096]{1,0:T(8,128)(2,1)} fusion(bf16[256,4096]{1,0:T(8,128)(2,1)} %fusion.8, s32[1024]{0:T(1024)S(1)} %pad_clamp_fusion), kind=kCustom, calls=%fused_computation | custom fusion | bytes 12585984 | tf_op jit(solution)/shard_map/jit(_take)/gather | solution.py:115
  252.4 3.9 select_select_fusion
  256.3 0.0 copy-start.5
  256.3 79.0 %all_to_all.10 = bf16[16,48,4096]{2,1,0:T(8,128)(2,1)S(1)} all-to-all(bf16[16,48,4096]{2,1,0:T(8,128)(2,1)S(1)} %select_select_fusion), channel_id=1, replica_groups=mesh['expert'=16,'tensor'=16] {'expert'}, dimensions={0} | all-to-all | bytes 12582912 | tf_op jit(solution)/shard_map/all_to_all | solution.py:117
  335.3 0.0 copy-done.5
  335.3 3.4 fusion.12
  338.7 0.0 copy-done.6
  338.7 3.5 fusion.22
  342.2 0.0 copy-done
  342.2 5.4 %convolution_convert_fusion = bf16[768,4096]{1,0:T(8,128)(2,1)} fusion(bf16[768,384]{1,0:T(8,128)(2,1)S(1)} %fusion.22, bf16[1,384,4096]{2,1,0:T(8,128)(2,1)S(1)} %copy-done), kind=kOutput, calls=%fused_computation.2 | convolution fusion | flops 2419064832 | bytes 10027008 | tf_op jit(solution)/shard_map/dot_general | solution.py:122
  347.6 6.0 %all-to-all-start.1 = ((bf16[16,48,4096]{2,1,0:T(8,128)(2,1)}), bf16[16,48,4096]{2,1,0:T(8,128)(2,1)}, u32[]{:S(2)}, u32[]{:S(2)}) async-start(bf16[16,48,4096]{2,1,0:T(8,128)(2,1)} %bitcast.108), calls=%async_computation.1 | async-start | bytes 12582912 | tf_op jit(solution)/shard_map/all_to_all | solution.py:124
  353.6 0.0 reduce-scatter.2.cloned.1.call-start
  353.6 0.0 copy-done.4
  353.7 0.0 copy-done.2
  353.7 0.1 select_reduce_fusion.1
  353.8 87.2 %all-to-all-done.1 = bf16[16,48,4096]{2,1,0:T(8,128)(2,1)} async-done(((bf16[16,48,4096]{2,1,0:T(8,128)(2,1)}), bf16[16,48,4096]{2,1,0:T(8,128)(2,1)}, u32[]{:S(2)}, u32[]{:S(2)}) %all-to-all-start.1) | async-done | bytes 6291488 | tf_op jit(solution)/shard_map/all_to_all | solution.py:124
  441.0 6.0 %fusion.3 = bf16[256,4096]{1,0:T(8,128)(2,1)} fusion(bf16[16,48,4096]{2,1,0:T(8,128)(2,1)} %all-to-all-done.1, bf16[256,16]{0,1:T(8,128)(2,1)S(1)} %bitcast.119, s32[256,16]{0,1:T(8,128)S(1)} %bitcast.113, pred[256,16]{0,1:T(8,128)(4,1)S(1)} %bitcast.118), kind=kOutput, calls=%fused_computation.11 | convolution fusion | flops 1612251136 | bytes 8417280 | tf_op jit(solution)/shard_map/njc,jcd->nd/dot_general | solution.py:126
  447.0 0.0 reduce-scatter.2.cloned.1.call-update
  447.0 65.0 %reduce-scatter.2.cloned.1.call-done = bf16[16,4096]{1,0:T(8,128)(2,1)} async-done(((bf16[256,4096]{1,0:T(8,128)(2,1)}), bf16[16,4096]{1,0:T(8,128)(2,1)}) %reduce-scatter.2.cloned.1.call-update) | async-done | bytes 131088 | tf_op jit(solution)/shard_map/reduce_scatter | solution.py:129
  512.0 1.7 add_convert_fusion.1
  (20 shorter events, 0.2 us)
Async XLA Ops:
  6.5 335.7 %copy-start = (bf16[1,384,4096]{2,1,0:T(8,128)(2,1)S(1)}, bf16[1,384,4096]{2,1,0:T(8,128)(2,1)}, u32[]{:S(2)}) copy-start(bf16[1,384,4096]{2,1,0:T(8,128)(2,1)} %param.21) | copy-start | bytes 9437188
  6.5 68.5 %all-gather.5.cloned.1.call-start = ((), (), s32[]{:S(2)}) async-start(), calls=%async_computation.4 | async-start | bytes 4456448 | tf_op jit(solution)/shard_map/all_gather | solution.py:87
  7.3 109.1 %all-gather.3.cloned.1.call-start = ((), (), s32[]{:S(2)}) async-start(), calls=%async_computation.3 | async-start | bytes 2228224 | tf_op jit(solution)/shard_map/all_gather | solution.py:106
  8.0 224.1 %all-reduce.2.cloned.1.call-start = ((), (), s32[]{:S(2)}) async-start(), calls=%async_computation.5 | async-start | bytes 4194304 | tf_op jit(solution)/shard_map/psum | solution.py:105
  79.8 156.8 %copy-start.3 = (f32[4096]{0:T(1024)S(1)}, f32[4096]{0:T(1024)}, u32[]{:S(2)}) copy-start(f32[4096]{0:T(1024)} %param.16) | copy-start | bytes 49156
  235.2 1.4 copy-start.1
  256.3 79.0 %copy-start.5 = (bf16[1,4096,384]{2,1,0:T(8,128)(2,1)S(1)}, bf16[1,4096,384]{2,1,0:T(8,128)(2,1)}, u32[]{:S(2)}) copy-start(bf16[1,4096,384]{2,1,0:T(8,128)(2,1)} %param.19) | copy-start | bytes 9437188
  335.3 3.4 copy-start.6
  347.6 6.0 %copy-start.4 = (bf16[256,8]{0,1:T(8,128)(2,1)S(1)}, bf16[256,8]{0,1:T(8,128)(2,1)}, u32[]{:S(2)}) copy-start(bf16[256,8]{0,1:T(8,128)(2,1)} %param.18) | copy-start | bytes 12292
  347.6 6.0 %copy-start.2 = (s32[256,8]{0,1:T(8,128)S(1)}, s32[256,8]{0,1:T(8,128)}, u32[]{:S(2)}) copy-start(s32[256,8]{0,1:T(8,128)} %param.17) | copy-start | bytes 24580
  347.6 93.4 %all-to-all-start.1 = ((bf16[16,48,4096]{2,1,0:T(8,128)(2,1)}), bf16[16,48,4096]{2,1,0:T(8,128)(2,1)}, u32[]{:S(2)}, u32[]{:S(2)}) async-start(bf16[16,48,4096]{2,1,0:T(8,128)(2,1)} %bitcast.108), calls=%async_computation.1 | async-start | bytes 12582912 | tf_op jit(solution)/shard_map/all_to_all | solution.py:124
  353.6 158.4 %reduce-scatter.2.cloned.1.call-start = ((), (), s32[]{:S(2)}) async-start(), calls=%async_computation.6 | async-start | bytes 2228224 | tf_op jit(solution)/shard_map/reduce_scatter | solution.py:129
Sparse Core Ops, SparseCore 0:
  9.8 65.2 all-gather.4
  76.8 39.4 all-gather.2
  118.7 113.3 all-reduce.1
  447.2 64.7 reduce-scatter.1
where the time goes:
time: 521 us; the launch traced here: 520 us
  waiting for transfers between devices  356 us (68%)
  blocking collectives  79 us (15%)
  matrix products  30.6 us (6%)
  local copies, waits for them, and re-layouts  20.5 us (4%)
  other arithmetic  14.3 us (3%)
  between operations  14 us (3%)
  starting transfers between devices  6.07 us (1%)
    psum x1, waiting for transfers between devices, shards(): lax.psum(head_part.astype(jnp.bfloat16), 'tensor').astype(jnp.float32)  116 us
    all_to_all x1, waiting for transfers between devices, shards(): lax.all_to_all(computed, 'expert', split_axis=0, concat_axis=0, tiled=True)  87.2 us
    all_to_all x1, blocking collectives, shards(): lax.all_to_all(outgoing, 'expert', split_axis=0, concat_axis=0, tiled=True)  79 us
    reduce_scatter x1, waiting for transfers between devices, shards(): lax.psum_scatter(expert_part.astype(jnp.bfloat16), 'tensor', scatter_dime...  65 us
    all_gather x1, waiting for transfers between devices, shards(): lax.all_gather(out_proj, 'expert', axis=1, tiled=True)  51.8 us
    all_gather x1, waiting for transfers between devices, shards(): residual_full = lax.all_gather(residual, 'tensor', axis=0, tiled=True)  34.7 us
    gather x1, local copies, waits for them, and re-layouts, shards(): jnp.take(normed_full, source_rows, axis=0)  13.8 us
  transfers between devices with their start and end apart: 5, of which 5 were waited for; matrix products, arithmetic and copies ran while one was open for 4% of the time, Pallas kernels for 0%

commit v1 on v0

--- a/solution.py
+++ b/solution.py
@@ -102,7 +102,9 @@
     slot_match = (hit_slot[:, :, None] == 1) & (
         position_slot[:, :, None] == jnp.arange(capacity, dtype=jnp.int32)[None, None, :]
     )
-    head_sum = lax.psum(head_part.astype(jnp.bfloat16), "tensor").astype(jnp.float32)
+    head_sum = jnp.sum(lax.all_gather(head_part.astype(jnp.bfloat16), "tensor"), axis=0).astype(
+        jnp.float32
+    )
     residual_full = lax.all_gather(residual, "tensor", axis=0, tiled=True)
     state_full = (residual_full.astype(jnp.float32) + head_sum).astype(jnp.bfloat16)
     hidden_state = lax.dynamic_slice_in_dim(state_full, start_row, TOK_DEV, 0)

time: 521 us -> 579 us (1.11)
  waiting for transfers between devices: 356 us -> 402 us
  other arithmetic: 14.3 us -> 25.7 us
    all_gather x0 -> x1, waiting for transfers between devices: none -> 170 us  [shards(): lax.all_gather(head_part.astype(jnp.bfloat16), 'tensor')]
    psum x1 -> x0, waiting for transfers between devices: 116 us -> none  [shards(): lax.psum(head_part.astype(jnp.bfloat16), 'tensor').astype(jnp.float32)]
    reduce_sum x0 -> x1, other arithmetic: none -> 13 us  [shards(): jnp.sum(lax.all_gather(head_part.astype(jnp.bfloat16), 'tensor'), axis=0)]
    all_gather x1, waiting for transfers between devices: 34.7 us -> 27.2 us  [shards(): residual_full = lax.all_gather(residual, 'tensor', axis=0, tiled=True)]
  transfers between devices with their start and end apart: 5 -> 5, of which waited for: 5 -> 5; matrix products, arithmetic and copies ran while one was open for 4% -> 5% of each run, Pallas kernels for 0% -> 0%
where the time goes in v1:
time: 579 us
  waiting for transfers between devices  402 us (69%)
  blocking collectives  79.7 us (14%)
  matrix products  30.6 us (5%)
  other arithmetic  25.7 us (4%)
  local copies, waits for them, and re-layouts  19.8 us (3%)
  between operations  14.2 us (2%)
  starting transfers between devices  6.25 us (1%)
    all_gather x1, waiting for transfers between devices, shards(): lax.all_gather(head_part.astype(jnp.bfloat16), 'tensor')  170 us
    all_to_all x1, waiting for transfers between devices, shards(): lax.all_to_all(computed, 'expert', split_axis=0, concat_axis=0, tiled=True)  88.4 us
    all_to_all x1, blocking collectives, shards(): lax.all_to_all(outgoing, 'expert', split_axis=0, concat_axis=0, tiled=True)  79.7 us
    reduce_scatter x1, waiting for transfers between devices, shards(): lax.psum_scatter(expert_part.astype(jnp.bfloat16), 'tensor', scatter_dime...  59.2 us
    all_gather x1, waiting for transfers between devices, shards(): lax.all_gather(out_proj, 'expert', axis=1, tiled=True)  56.4 us
    all_gather x1, waiting for transfers between devices, shards(): residual_full = lax.all_gather(residual, 'tensor', axis=0, tiled=True)  27.2 us
    gather x1, local copies, waits for them, and re-layouts, shards(): jnp.take(normed_full, source_rows, axis=0)  13.8 us
    reduce_sum x1, other arithmetic, shards(): jnp.sum(lax.all_gather(head_part.astype(jnp.bfloat16), 'tensor'), axis=0)  13 us
  transfers between devices with their start and end apart: 5, of which 5 were waited for; matrix products, arithmetic and copies ran while one was open for 5% of the time, Pallas kernels for 0%

profile of v1, /device:TPU:2, one launch (start us, length us, event | category | flops | bytes accessed | tf_op | source)
XLA Modules:
  0.0 578.7 jit_solution(2232472187698977132)
XLA Ops:
  6.5 0.0 copy-start
  6.5 0.0 all-gather.7.cloned.1.call-start
  6.5 0.7 all-gather.7.cloned.1.call-update
  7.3 0.0 all-gather.9.cloned.1.call-start
  8.2 2.0 dynamic-slice_bitcast_fusion
  10.1 1.0 fusion.26
  11.2 5.1 fusion.62
  16.2 2.4 fusion.33
  18.6 56.4 %all-gather.7.cloned.1.call-done = bf16[512,4096]{1,0:T(8,128)(2,1)} async-done(((bf16[512,256]{1,0:T(8,128)(2,1)}), bf16[512,4096]{1,0:T(8,128)(2,1)}) %all-gather.7.cloned.1.call-update) | async-done | bytes 4194320 | tf_op jit(solution)/shard_map/all_gather | solution.py:87
  75.0 4.8 convolution_convert_fusion.1
  79.9 0.0 all-gather.9.cloned.1.call-update
  79.9 0.2 all-gather.5.cloned.1.call-start
  80.1 0.5 all-gather.5.cloned.1.call-update
  80.6 0.0 copy-done.2
  80.7 0.1 convert_reduce_fusion
  80.7 0.1 copy.36
  80.9 1.1 copy.38
  82.0 1.3 reduce_window_sum.14
  83.4 0.4 select_reduce_fusion
  83.8 0.1 reshape.155
  83.8 0.4 fusion.37
  84.2 170.0 %all-gather.9.cloned.1.call-done = bf16[4096,4096]{1,0:T(8,128)(2,1)} async-done(((bf16[256,4096]{1,0:T(8,128)(2,1)}), bf16[4096,4096]{1,0:T(8,128)(2,1)}) %all-gather.9.cloned.1.call-update) | async-done | bytes 33554448 | tf_op jit(solution)/shard_map/all_gather | solution.py:105
  254.2 13.0 %reduce_sum.60 = bf16[256,4096]{1,0:T(8,128)(2,1)} reduce(bf16[16,256,4096]{2,1,0:T(8,128)(2,1)} %bitcast.108, bf16[]{:T(256)} %constant.95.clone.1), dimensions={0}, to_apply=%region_2.3 | reduce | flops 15728640 | bytes 35651584 | tf_op jit(solution)/shard_map/reduce_sum | solution.py:105
  267.2 27.2 %all-gather.5.cloned.1.call-done = bf16[256,4096]{1,0:T(8,128)(2,1)} async-done(((bf16[16,4096]{1,0:T(8,128)(2,1)}), bf16[256,4096]{1,0:T(8,128)(2,1)}) %all-gather.5.cloned.1.call-update) | async-done | bytes 2097168 | tf_op jit(solution)/shard_map/all_gather | solution.py:108
  294.4 3.2 fusion.6
  297.5 0.0 copy-start.1
  297.6 1.3 copy-done.1
  298.9 0.0 copy-done.3
  298.9 2.0 fusion.8
  300.9 13.8 %gather_fusion = bf16[768,4096]{1,0:T(8,128)(2,1)} fusion(bf16[256,4096]{1,0:T(8,128)(2,1)} %fusion.8, s32[1024]{0:T(1024)S(1)} %pad_clamp_fusion), kind=kCustom, calls=%fused_computation | custom fusion | bytes 12585984 | tf_op jit(solution)/shard_map/jit(_take)/gather | solution.py:117
  314.7 3.9 select_select_fusion
  318.6 0.0 copy-start.5
  318.6 79.7 %all_to_all.10 = bf16[16,48,4096]{2,1,0:T(8,128)(2,1)S(1)} all-to-all(bf16[16,48,4096]{2,1,0:T(8,128)(2,1)S(1)} %select_select_fusion), channel_id=1, replica_groups=mesh['expert'=16,'tensor'=16] {'expert'}, dimensions={0} | all-to-all | bytes 12582912 | tf_op jit(solution)/shard_map/all_to_all | solution.py:119
  398.3 0.0 copy-done.5
  398.3 3.4 fusion.12
  401.8 0.0 copy-done.6
  401.8 3.5 fusion.22
  405.2 0.0 copy-done
  405.3 5.4 convolution_convert_fusion
  410.7 6.0 %all-to-all-start.1 = ((bf16[16,48,4096]{2,1,0:T(8,128)(2,1)}), bf16[16,48,4096]{2,1,0:T(8,128)(2,1)}, u32[]{:S(2)}, u32[]{:S(2)}) async-start(bf16[16,48,4096]{2,1,0:T(8,128)(2,1)} %bitcast.110), calls=%async_computation.1 | async-start | bytes 12582912 | tf_op jit(solution)/shard_map/all_to_all | solution.py:126
  416.6 0.0 reduce-scatter.2.cloned.1.call-start
  416.7 0.0 copy-done.4
  416.7 0.1 select_reduce_fusion.1
  416.8 88.4 %all-to-all-done.1 = bf16[16,48,4096]{2,1,0:T(8,128)(2,1)} async-done(((bf16[16,48,4096]{2,1,0:T(8,128)(2,1)}), bf16[16,48,4096]{2,1,0:T(8,128)(2,1)}, u32[]{:S(2)}, u32[]{:S(2)}) %all-to-all-start.1) | async-done | bytes 6291488 | tf_op jit(solution)/shard_map/all_to_all | solution.py:126
  505.3 6.0 %fusion.3 = bf16[256,4096]{1,0:T(8,128)(2,1)} fusion(bf16[16,48,4096]{2,1,0:T(8,128)(2,1)} %all-to-all-done.1, bf16[256,16]{0,1:T(8,128)(2,1)S(1)} %bitcast.121, s32[256,16]{0,1:T(8,128)S(1)} %bitcast.115, pred[256,16]{0,1:T(8,128)(4,1)S(1)} %bitcast.120), kind=kOutput, calls=%fused_computation.11 | convolution fusion | flops 1612251136 | bytes 8417280 | tf_op jit(solution)/shard_map/njc,jcd->nd/dot_general | solution.py:128
  511.3 0.0 reduce-scatter.2.cloned.1.call-update
  511.3 59.2 %reduce-scatter.2.cloned.1.call-done = bf16[16,4096]{1,0:T(8,128)(2,1)} async-done(((bf16[256,4096]{1,0:T(8,128)(2,1)}), bf16[16,4096]{1,0:T(8,128)(2,1)}) %reduce-scatter.2.cloned.1.call-update) | async-done | bytes 131088 | tf_op jit(solution)/shard_map/reduce_scatter | solution.py:131
  570.5 1.7 add_convert_fusion.1
  (21 shorter events, 0.3 us)
Async XLA Ops:
  6.5 398.7 %copy-start = (bf16[1,384,4096]{2,1,0:T(8,128)(2,1)S(1)}, bf16[1,384,4096]{2,1,0:T(8,128)(2,1)}, u32[]{:S(2)}) copy-start(bf16[1,384,4096]{2,1,0:T(8,128)(2,1)} %param.21) | copy-start | bytes 9437188
  6.5 68.5 %all-gather.7.cloned.1.call-start = ((), (), s32[]{:S(2)}) async-start(), calls=%async_computation.4 | async-start | bytes 4456448 | tf_op jit(solution)/shard_map/all_gather | solution.py:87
  7.3 246.9 %all-gather.9.cloned.1.call-start = ((), (), s32[]{:S(2)}) async-start(), calls=%async_computation.6 | async-start | bytes 35651584 | tf_op jit(solution)/shard_map/all_gather | solution.py:105
  75.0 5.6 copy-start.2
  79.9 214.5 %all-gather.5.cloned.1.call-start = ((), (), s32[]{:S(2)}) async-start(), calls=%async_computation.3 | async-start | bytes 2228224 | tf_op jit(solution)/shard_map/all_gather | solution.py:108
  267.2 31.7 %copy-start.3 = (f32[4096]{0:T(1024)S(1)}, f32[4096]{0:T(1024)}, u32[]{:S(2)}) copy-start(f32[4096]{0:T(1024)} %param.16) | copy-start | bytes 49156
  297.5 1.4 copy-start.1
  318.6 79.7 %copy-start.5 = (bf16[1,4096,384]{2,1,0:T(8,128)(2,1)S(1)}, bf16[1,4096,384]{2,1,0:T(8,128)(2,1)}, u32[]{:S(2)}) copy-start(bf16[1,4096,384]{2,1,0:T(8,128)(2,1)} %param.19) | copy-start | bytes 9437188
  398.3 3.4 copy-start.6
  410.7 6.0 %copy-start.4 = (bf16[256,8]{0,1:T(8,128)(2,1)S(1)}, bf16[256,8]{0,1:T(8,128)(2,1)}, u32[]{:S(2)}) copy-start(bf16[256,8]{0,1:T(8,128)(2,1)} %param.18) | copy-start | bytes 12292
  410.7 94.6 %all-to-all-start.1 = ((bf16[16,48,4096]{2,1,0:T(8,128)(2,1)}), bf16[16,48,4096]{2,1,0:T(8,128)(2,1)}, u32[]{:S(2)}, u32[]{:S(2)}) async-start(bf16[16,48,4096]{2,1,0:T(8,128)(2,1)} %bitcast.110), calls=%async_computation.1 | async-start | bytes 12582912 | tf_op jit(solution)/shard_map/all_to_all | solution.py:126
  416.6 153.9 %reduce-scatter.2.cloned.1.call-start = ((), (), s32[]{:S(2)}) async-start(), calls=%async_computation.5 | async-start | bytes 2228224 | tf_op jit(solution)/shard_map/reduce_scatter | solution.py:131
Sparse Core Ops, SparseCore 0:
  9.8 65.2 all-gather.6
  80.0 174.1 all-gather.8
  256.0 38.3 all-gather.4
  511.4 59.0 reduce-scatter.1
